TPU v7x, 128 devices: a whole 4x4x4 slice. The times are simulated.
128 devices in a mesh: bx: 16 (over x, z), by: 8 (over y, core).
Axes of the slice: x: 4, y: 4, z: 4, core: 2. Of those that a mesh axis runs over, the one named last changes fastest.
Arguments:
- features: bfloat16 [16, 8, 1024, 128], P('bx', 'by'), may hold values from -13 to 13
- live_count: int32 [16, 8], P('bx', 'by'), may hold values from 128 to 1024, as said below
- neighbour_map: int32 [16, 8, 27, 1024], P('bx', 'by'), may hold values from 0 to 2175, as said below
- send_rows: int32 [16, 8, 8, 128], P('bx', 'by'), may hold values from 0 to 1023, as said below
- weight: bfloat16 [3456, 128], replicated, may hold values from -0.109375 to 0.109375
- gain: float32 [128], replicated, may hold values from 0.5 to 1.5
- shift: float32 [128], replicated, may hold values from -3 to 3
- cotangent: bfloat16 [16, 8, 1024, 128], P('bx', 'by'), may hold values from -13 to 13
Outputs:
- activated: bfloat16 [16, 8, 1024, 128], P('bx', 'by')
- grad_features: bfloat16 [16, 8, 1024, 128], P('bx', 'by')
- grad_weight: float32 [27, 128, 128], P(None, 'bx', 'by')
Inputs may be any that keep to these rules, and one draw needn't show every extreme that they name: Rows 0 to live_count - 1 of a brick are live, the rest padding; in every draw some brick is full. `send_rows`: every entry is below its brick's live count; the eight blocks follow the directions (dx, dy) in row-major order with the brick's own position left out. `neighbour_map`: entries index the brick's extended table; offset 13 of a live row names that row itself; every entry of a padding row is 1536. With B = min(1024, 512) and q = r // B for a live row r, an entry below 1024 lies in rows q B to q B + B - 1, and an entry 1024 + b * 128 + h of incoming block b other than 4 has h in q * 128 B / 1024 to (q + 1) * 128 B / 1024 - 1.
All inputs are finite; a program needn't handle non-finite values.
Results may differ from a plain program's by a relative error of at most 0.029.
The roundings to bfloat16 on the way count: a program that leaves them out, or rounds other values in their place, can miss the bound.
Values may be sent and summed in bfloat16 or wider, within the bound.
No kernel may reach another device: no remote copies, remote signals or barrier semaphores. Data moves between devices by JAX's collectives and lax.ppermute only.
A program may use at most 64 MiB of HBM per device.

v0:
```python
import jax
import jax.numpy as jnp
from jax import lax
from jax.sharding import PartitionSpec as P

epsilon = 1e-05


def extended(cells, sides, width):
    for axis, dim in sides:
        count = lax.axis_size(axis)
        ends = count - 1
        head = lax.slice_in_dim(cells, 0, width, axis=dim)
        tail = lax.slice_in_dim(cells, cells.shape[dim] - width, cells.shape[dim], axis=dim)
        cells = jnp.concatenate(
            [
                lax.ppermute(tail, axis, [(i, (i + 1) % count) for i in range(ends)]),
                cells,
                lax.ppermute(head, axis, [((i + 1) % count, i) for i in range(ends)]),
            ],
            axis=dim,
        )
    return cells


def from_neighbours(outgoing):
    padded = extended(outgoing, (("bx", 0), ("by", 1)), 1)
    return padded[::2, ::2]


def per_device(features, live_count, neighbour_map, send_rows, weight, gain, shift, cotangent):
    own_rows = features[0, 0]
    rows_total, channels = own_rows.shape
    halo_rows = send_rows.shape[3]
    block_rows = min(rows_total, 512)
    blocks_count = rows_total // block_rows
    halo_window = halo_rows // blocks_count
    window_rows = block_rows + 9 * halo_window
    sent_index = send_rows[0, 0].reshape(-1)
    send_select = (
        sent_index[:, None] == lax.broadcasted_iota(jnp.int32, (1, rows_total), 1)
    ).astype(jnp.bfloat16)
    chosen_rows = jnp.dot(send_select, own_rows, preferred_element_type=jnp.float32).astype(
        jnp.bfloat16
    )
    chosen_rows = chosen_rows.reshape(8, halo_rows, channels)
    blank_block = jnp.zeros((1, halo_rows, channels), jnp.bfloat16)
    outgoing = jnp.concatenate([chosen_rows[:4], blank_block, chosen_rows[4:]], axis=0).reshape(
        3, 3, halo_rows, channels
    )
    incoming = from_neighbours(outgoing).reshape(9, blocks_count, halo_window, channels)
    index_blocks = neighbour_map[0, 0].reshape(27, blocks_count, block_rows).transpose(1, 0, 2)
    own_blocks = own_rows.reshape(blocks_count, block_rows, channels)
    halo_blocks = incoming.transpose(1, 0, 2, 3)
    block_ids = jnp.arange(blocks_count, dtype=jnp.int32)

    def selector_of(indices, block_index):
        beyond = indices - rows_total
        target = beyond // halo_rows
        inside = beyond - target * halo_rows - block_index * halo_window
        local_pos = indices - block_index * block_rows
        remote_pos = block_rows + target * halo_window + inside
        usable = (inside >= 0) & (inside < halo_window)
        position = jnp.where(indices < rows_total, local_pos, jnp.where(usable, remote_pos, -1))
        return position[:, :, None] == lax.broadcasted_iota(jnp.int32, (1, 1, window_rows), 2)

    def forward_block(pieces):
        indices, own_part, halo_part, block_index = pieces
        window = jnp.concatenate([own_part, halo_part.reshape(9 * halo_window, channels)], axis=0)
        selector = selector_of(indices, block_index).astype(jnp.bfloat16)
        gathered = jnp.einsum(
            "kbw,wc->bkc", selector, window, preferred_element_type=jnp.float32
        ).astype(jnp.bfloat16)
        columns = gathered.reshape(block_rows, 27 * channels)
        return (jnp.dot(columns, weight, preferred_element_type=jnp.float32), columns)

    conv_blocks, column_blocks = lax.map(
        forward_block, (index_blocks, own_blocks, halo_blocks, block_ids)
    )
    conv_out = conv_blocks.reshape(rows_total, channels).astype(jnp.bfloat16)
    conv_float = conv_out.astype(jnp.float32)
    live_mask = (lax.broadcasted_iota(jnp.int32, (rows_total, 1), 0) < live_count[0, 0]).astype(
        jnp.float32
    )
    local_count = jnp.sum(live_mask)
    total_sum, total_count = lax.psum(
        (jnp.sum(conv_float * live_mask, axis=0), local_count), ("bx", "by")
    )
    center = total_sum / total_count
    deviation = (conv_float - center) * live_mask
    variance = lax.psum(jnp.sum(deviation * deviation, axis=0), ("bx", "by")) / total_count
    inverse_std = lax.rsqrt(variance + epsilon)
    normalized = (conv_float - center) * inverse_std
    before = gain * normalized + shift
    activated = (jnp.maximum(before, 0.0) * live_mask).astype(jnp.bfloat16)
    upstream = cotangent[0, 0].astype(jnp.float32) * (before > 0.0) * live_mask
    sum_up, sum_cross = lax.psum(
        (jnp.sum(upstream, axis=0), jnp.sum(upstream * normalized, axis=0)), ("bx", "by")
    )
    conv_grad = (
        gain
        * inverse_std
        * (upstream - live_mask * (sum_up + normalized * sum_cross) / total_count)
    ).astype(jnp.bfloat16)
    grad_blocks = conv_grad.reshape(blocks_count, block_rows, channels)

    def backward_block(weight_acc, pieces):
        indices, columns, grad_rows, block_index = pieces
        weight_acc = weight_acc + lax.dot_general(
            columns, grad_rows, (((0,), (0,)), ((), ())), preferred_element_type=jnp.float32
        )
        column_grad = lax.dot_general(
            grad_rows, weight, (((1,), (1,)), ((), ())), preferred_element_type=jnp.float32
        )
        column_grad = column_grad.reshape(block_rows, 27, channels)
        selector = selector_of(indices, block_index).astype(jnp.float32)
        window_grad = jnp.einsum(
            "kbw,bkc->wc",
            selector,
            column_grad,
            precision=lax.Precision.HIGHEST,
            preferred_element_type=jnp.float32,
        )
        return (
            weight_acc,
            (window_grad[:block_rows], window_grad[block_rows:].reshape(9, halo_window, channels)),
        )

    start_acc = jnp.zeros((27 * channels, channels), jnp.float32)
    weight_acc, (own_parts, halo_parts) = lax.scan(
        backward_block, start_acc, (index_blocks, column_blocks, grad_blocks, block_ids)
    )
    weight_terms = weight_acc.reshape(27, channels, channels)
    partial_x = lax.psum_scatter(
        weight_terms.astype(jnp.bfloat16), "bx", scatter_dimension=1, tiled=True
    )
    summed = lax.psum_scatter(partial_x, "by", scatter_dimension=2, tiled=True).astype(jnp.float32)
    grad_weight = summed / jnp.sqrt(total_count)
    own_table = own_parts.reshape(rows_total, channels)
    halo_table = halo_parts.transpose(1, 0, 2, 3).reshape(3, 3, halo_rows, channels)
    halo_grad = halo_table.astype(jnp.bfloat16)
    returned = from_neighbours(halo_grad).reshape(9, halo_rows, channels)
    slots_back = (
        jnp.concatenate([returned[:4], returned[5:]], axis=0)
        .reshape(-1, channels)
        .astype(jnp.float32)
    )
    added_back = lax.dot_general(
        send_select.astype(jnp.float32),
        slots_back,
        (((0,), (0,)), ((), ())),
        precision=lax.Precision.HIGHEST,
        preferred_element_type=jnp.float32,
    )
    own_grad = own_table + added_back
    return (activated[None, None], own_grad.astype(jnp.bfloat16)[None, None], grad_weight)


def solution(mesh):
    return jax.shard_map(
        per_device,
        mesh=mesh,
        in_specs=(
            P("bx", "by", None, None),
            P("bx", "by"),
            P("bx", "by", None, None),
            P("bx", "by", None, None),
            P(),
            P(),
            P(),
            P("bx", "by", None, None),
        ),
        out_specs=(P("bx", "by", None, None), P("bx", "by", None, None), P(None, "bx", "by")),
        check_vma=False,
    )
```

profile of v0, /device:TPU:0, one launch (start us, length us, event | category | flops | bytes accessed | tf_op | source)
XLA Modules:
  0.0 465.1 jit_solution(409183118276341036)
XLA Ops:
  7.2 1.9 fusion.34
  9.1 3.9 collective-permute-start
  13.0 1.3 collective-permute-start.1
  15.2 4.3 collective-permute-done.1
  19.5 0.8 pad_maximum_fusion.9
  20.3 1.9 collective-permute-start.2
  22.2 1.3 collective-permute-start.3
  23.6 1.2 reduce.4
  24.7 0.1 reshape_squeeze.7
  24.9 0.6 fusion.44
  25.5 1.5 collective-permute-done.3
  27.0 1.1 pad_maximum_fusion
  28.2 38.2 %while.33 = (s32[]{:T(128)}, bf16[2,512,128]{2,1,0:T(8,128)(2,1)S(1)}, bf16[2,512,3456]{1,2,0:T(8,128)(2,1)}, bf16[2,512,128]{2,1,0:T(8,128)(2,1)}, bf16[2,9,64,...) while((s32[]{:T(128)}, ...), condition=%wide.region_1.2_spmd.clone, body=%wide.region_0.1_spmd.sunk.clone | while | flops 4321123840 | bytes 16304801 | solution.py:77
  28.2 0.6 dynamic_slice.94
  30.2 0.9 dynamic-slice_bitcast_fusion.3
  31.2 13.0 %fusion.82 = bf16[128,27,512]{2,0,1:T(8,128)(2,1)S(1)} fusion(s32[27,512]{1,0:T(8,128)S(1)} %bitcast_select_fusion.6, bf16[576,128]{1,0:T(8,128)(2,1)S(1)} %bitcast.223, bf16[512,128]{1,0:T(8,128)(2,1)S(1)} %dynamic-slice_bitcast_fusion.3), kind=kOutput, calls=%fused_computation.3.clone.1.clone | convolution fusion | flops 3867738112 | bytes 3872768 | tf_op jit(solution)/shard_map/while/body/eval_jaxpr/kbw,wc->bkc/dot_general | solution.py:71
  44.1 2.0 constant_dynamic-update-slice_fusion.6
  46.1 1.2 fusion.83
  47.3 0.6 dynamic_slice.94
  49.3 0.9 dynamic-slice_bitcast_fusion.3
  50.2 13.0 %fusion.82 = bf16[128,27,512]{2,0,1:T(8,128)(2,1)S(1)} fusion(s32[27,512]{1,0:T(8,128)S(1)} %bitcast_select_fusion.6, bf16[576,128]{1,0:T(8,128)(2,1)S(1)} %bitcast.223, bf16[512,128]{1,0:T(8,128)(2,1)S(1)} %dynamic-slice_bitcast_fusion.3), kind=kOutput, calls=%fused_computation.3.clone.1.clone | convolution fusion | flops 3867738112 | bytes 3872768 | tf_op jit(solution)/shard_map/while/body/eval_jaxpr/kbw,wc->bkc/dot_general | solution.py:71
  63.2 2.0 constant_dynamic-update-slice_fusion.6
  65.2 1.2 fusion.83
  66.4 0.2 multiply_reduce_fusion.1
  66.6 70.3 %all-reduce.2 = (f32[128]{0:T(128)S(1)}, f32[]{:T(128)}) all-reduce(f32[128]{0:T(128)S(1)} %multiply_reduce_fusion.1, f32[]{:T(128)} %fusion.44), channel_id=1, replica_groups=mesh['bx'=16,'by'=8] {'bx','by'}, use_global_device_ids=true, to_apply=%region_3.4 | all-reduce | flops 129 | bytes 1032 | tf_op jit(solution)/shard_map/psum | solution.py:86
  136.9 0.7 broadcast_divide_fusion
  137.6 0.2 multiply_reduce_fusion
  137.8 62.7 %psum.37 = f32[128]{0:T(128)S(1)} all-reduce(f32[128]{0:T(128)S(1)} %multiply_reduce_fusion), channel_id=1, replica_groups=mesh['bx'=16,'by'=8] {'bx','by'}, use_global_device_ids=true, to_apply=%region_7.8 | all-reduce | flops 128 | bytes 1024 | tf_op jit(solution)/shard_map/psum | solution.py:91
  200.5 0.7 fusion.46
  201.2 1.2 fusion.39
  202.4 64.2 %all-reduce.1 = (f32[128]{0:T(128)S(1)}, f32[128]{0:T(128)S(1)}) all-reduce(f32[128]{0:T(128)S(1)} %get-tuple-element.329, f32[128]{0:T(128)S(1)} %get-tuple-element.328), channel_id=1, replica_groups=mesh['bx'=16,'by'=8] {'bx','by'}, use_global_device_ids=true, to_apply=%region_11.12 | all-reduce | flops 256 | bytes 2048 | tf_op jit(solution)/shard_map/psum | solution.py:97
  266.6 1.9 fusion.42
  268.5 73.1 %while.34 = (s32[]{:T(128)}, f32[3456,128]{1,0:T(8,128)S(1)}, f32[2,512,128]{2,1,0:T(8,128)}, bf16[2,9,64,128]{3,2,0,1:T(8,128)(2,1)}, bf16[2,512,3456]{1,2,0:T(...) while((s32[]{:T(128)}, f32[3456,128]{1,0:T(8,128)S(1)}, ...), condition=%wide.region_13.14_spmd.clone.clone, body=%wide.region_12.13_spmd.clone.sunk.clone | while | flops 24024522752 | bytes 28413672 | solution.py:130
  268.5 0.6 dynamic_slice.99
  270.5 1.1 fusion.89
  271.6 28.7 %fusion.90 = f32[1088,128]{1,0:T(8,128)S(1)} fusion(f32[512,27,128]{2,0,1:T(8,128)S(1)} %fusion.89, s32[27,512]{1,0:T(8,128)S(1)} %bitcast_select_fusion.7), kind=kOutput, calls=%fused_computation.31.clone.1.clone | convolution fusion | flops 23117266944 | bytes 7690240 | tf_op jit(solution)/shard_map/while/body/eval_jaxpr/kbw,bkc->wc/dot_general | solution.py:117
  300.4 0.8 copy-done.4
  301.1 0.7 constant_dynamic-update-slice_fusion.7
  301.8 3.2 convolution_add_fusion.3
  305.1 0.6 dynamic_slice.99
  307.1 1.1 fusion.89
  308.2 28.7 %fusion.90 = f32[1088,128]{1,0:T(8,128)S(1)} fusion(f32[512,27,128]{2,0,1:T(8,128)S(1)} %fusion.89, s32[27,512]{1,0:T(8,128)S(1)} %bitcast_select_fusion.7), kind=kOutput, calls=%fused_computation.31.clone.1.clone | convolution fusion | flops 23117266944 | bytes 7690240 | tf_op jit(solution)/shard_map/while/body/eval_jaxpr/kbw,bkc->wc/dot_general | solution.py:117
  337.0 0.8 copy-done.4
  337.7 0.7 constant_dynamic-update-slice_fusion.7
  338.4 3.2 convolution_add_fusion.3
  341.7 1.0 convert_element_type.131
  342.8 1.0 fusion.48
  343.7 1.3 collective-permute-start.4
  345.0 1.3 collective-permute-start.5
  346.4 0.6 dynamic-slice
  348.3 4.0 collective-permute-done.5
  352.3 1.0 pad_maximum_fusion.6
  353.3 1.5 collective-permute-start.6
  354.8 1.3 collective-permute-start.7
  356.1 0.9 multiply_convert_fusion
  357.1 2.2 collective-permute-done.7
  359.3 1.1 pad_maximum_fusion.1
  360.5 64.4 %all-reduce.5.cloned.1.call-done = bf16[27,128,128]{2,1,0:T(8,128)(2,1)} async-done(((bf16[27,128,128]{2,1,0:T(8,128)(2,1)}), bf16[27,128,128]{2,1,0:T(8,128)(2,1)}) %all-reduce.5.cloned.1.call-update) | async-done | bytes 884752
  424.9 0.8 constant_dynamic-slice_fusion.1
  425.7 0.9 copy.30
  426.7 3.2 fusion.35
  429.9 27.0 %reduce-scatter.3.cloned.1.call-done = bf16[27,8,16]{0,1,2:T(8,128)(2,1)} async-done(((bf16[27,8,128]{0,1,2:T(8,128)(2,1)}), bf16[27,8,16]{0,1,2:T(8,128)(2,1)}) %reduce-scatter.3.cloned.1.call-update) | async-done | bytes 6928 | tf_op jit(solution)/shard_map/reduce_scatter | solution.py:137
  456.9 0.8 convert_divide_fusion
  457.6 0.6 copy.31
  (52 shorter events, 1.0 us)
Async XLA Ops:
  7.2 21.0 %copy-start = (bf16[3456,128]{1,0:T(8,128)(2,1)S(1)}, bf16[3456,128]{1,0:T(8,128)(2,1)}, u32[]{:S(2)}) copy-start(bf16[3456,128]{1,0:T(8,128)(2,1)} %param.16) | copy-start | bytes 2654212
  7.2 417.8 %all-reduce.5.cloned.1.call-start = ((), (), s32[]{:S(2)}) async-start(), calls=%async_computation.2 | async-start | bytes 1769472
  9.1 6.1 %collective-permute-start = (bf16[1,3,128,128]{3,2,1,0:T(8,128)(2,1)S(1)}, bf16[1,3,128,128]{3,2,1,0:T(8,128)(2,1)S(1)}, u32[]{:S(2)}, u32[]{:S(2)}) collective-permute-start(bf16[1,3,128,128]{3,2,1,0:T(8,128)(2,1)S(1)} %bitcast.239), channel_id=1, source_target_pairs={{0,8},{8,16},{16,24},{24,32},{32,40},{40,48},{48,56},{56,64},{64,7... | collective-permute-start | bytes 294920 | tf_op jit(solution)/shard_map/ppermute | solution.py:17
  13.0 6.5 %collective-permute-start.1 = (bf16[1,3,128,128]{3,2,1,0:T(8,128)(2,1)S(1)}, bf16[1,3,128,128]{3,2,1,0:T(8,128)(2,1)S(1)}, u32[]{:S(2)}, u32[]{:S(2)}) collective-permute-start(bf16[1,3,128,128]{3,2,1,0:T(8,128)(2,1)S(1)} %bitcast.238), channel_id=1, source_target_pairs={{8,0},{16,8},{24,16},{32,24},{40,32},{48,40},{56,48},{64,56},{72,6... | collective-permute-start | bytes 294920 | tf_op jit(solution)/shard_map/ppermute | solution.py:19
  20.3 5.2 %collective-permute-start.2 = (bf16[5,1,128,128]{3,2,1,0:T(8,128)(2,1)}, bf16[5,1,128,128]{3,2,1,0:T(8,128)(2,1)}, u32[]{:S(2)}, u32[]{:S(2)}) collective-permute-start(bf16[5,1,128,128]{3,2,1,0:T(8,128)(2,1)} %get-tuple-element.372), channel_id=1, source_target_pairs={{0,1},{1,2},{2,3},{3,4},{4,5},{5,6},{6,7},{8,9},{9,10},{10,11},{11... | collective-permute-start | bytes 491528 | tf_op jit(solution)/shard_map/ppermute | solution.py:17
  22.2 4.8 %collective-permute-start.3 = (bf16[5,1,128,128]{3,2,1,0:T(8,128)(2,1)}, bf16[5,1,128,128]{3,2,1,0:T(8,128)(2,1)}, u32[]{:S(2)}, u32[]{:S(2)}) collective-permute-start(bf16[5,1,128,128]{3,2,1,0:T(8,128)(2,1)} %get-tuple-element.373), channel_id=1, source_target_pairs={{1,0},{2,1},{3,2},{4,3},{5,4},{6,5},{7,6},{9,8},{10,9},{11,10},{12... | collective-permute-start | bytes 491528 | tf_op jit(solution)/shard_map/ppermute | solution.py:19
  28.2 172.3 %copy-start.1 = (f32[128]{0:T(128)S(1)}, f32[128]{0:T(128)}, u32[]{:S(2)}) copy-start(f32[128]{0:T(128)} %param.17) | copy-start | bytes 1540
  28.2 173.0 %copy-start.2 = (f32[128]{0:T(128)S(1)}, f32[128]{0:T(128)}, u32[]{:S(2)}) copy-start(f32[128]{0:T(128)} %param.18) | copy-start | bytes 1540
  268.5 77.9 %copy-start.6 = (u32[128]{0:T(128)S(1)}, u32[128]{0:T(128)}, u32[]{:S(2)}) copy-start(u32[128]{0:T(128)} %constant.182) | copy-start | bytes 1540
  271.6 28.7 %copy-start.3 = (f32[2,512,128]{2,1,0:T(8,128)S(1)}, f32[2,512,128]{2,1,0:T(8,128)}, u32[]{:S(2)}) copy-start(f32[2,512,128]{2,1,0:T(8,128)} %get-tuple-element.580) | copy-start | bytes 1572868 | tf_op jit(solution)/shard_map/while
  300.4 0.8 copy-start.4
  308.1 28.7 %copy-start.3 = (f32[2,512,128]{2,1,0:T(8,128)S(1)}, f32[2,512,128]{2,1,0:T(8,128)}, u32[]{:S(2)}) copy-start(f32[2,512,128]{2,1,0:T(8,128)} %get-tuple-element.580) | copy-start | bytes 1572868 | tf_op jit(solution)/shard_map/while
  336.9 0.8 copy-start.4
  341.6 85.0 %copy-start.5 = (s32[1,1,8,128]{3,2,1,0:T(8,128)S(1)}, s32[1,1,8,128]{3,2,1,0:T(8,128)}, u32[]{:S(2)}) copy-start(s32[1,1,8,128]{3,2,1,0:T(8,128)} %param.15) | copy-start | bytes 12292
  342.7 114.2 %reduce-scatter.3.cloned.1.call-start = ((), (), s32[]{:S(2)}) async-start(), calls=%async_computation.1 | async-start | bytes 294912 | tf_op jit(solution)/shard_map/reduce_scatter | solution.py:137
  343.7 4.6 collective-permute-start.4
  345.0 7.3 %collective-permute-start.5 = (bf16[1,3,128,128]{3,2,1,0:T(8,128)(2,1)S(1)}, bf16[1,3,128,128]{3,2,1,0:T(8,128)(2,1)S(1)}, u32[]{:S(2)}, u32[]{:S(2)}) collective-permute-start(bf16[1,3,128,128]{3,2,1,0:T(8,128)(2,1)S(1)} %bitcast.236), channel_id=1, source_target_pairs={{8,0},{16,8},{24,16},{32,24},{40,32},{48,40},{56,48},{64,56},{72,6... | collective-permute-start | bytes 294920 | tf_op jit(solution)/shard_map/ppermute | solution.py:19
  353.3 3.7 collective-permute-start.6
  354.8 4.5 collective-permute-start.7
Sparse Core Ops, SparseCore 0:
  342.8 82.0 all-reduce.4
  427.3 29.5 reduce-scatter.2
where the time goes:
time: 466 us; the launch traced here: 465 us
  blocking collectives  197 us (42%)
  waiting for transfers between devices  104 us (22%)
  matrix products  99.4 us (21%)
  between operations  16.4 us (4%)
  local copies, waits for them, and re-layouts  15.4 us (3%)
  starting transfers between devices  13.9 us (3%)
  other arithmetic  13.7 us (3%)
  loops' own time  5.44 us (1%)
    psum x1, blocking collectives, per_device(): lax.psum((jnp.sum(conv_float * live_mask, axis=0), local_count), ('bx', '...  70.3 us
    unnamed x3, waiting for transfers between devices  64.5 us
    psum x1, blocking collectives, per_device(): lax.psum((jnp.sum(upstream, axis=0), jnp.sum(upstream * normalized, axis=...  64.2 us
    psum x1, blocking collectives, per_device(): lax.psum(jnp.sum(deviation * deviation, axis=0), ('bx', 'by')) / total_count  62.7 us
    dot_general x2, matrix products, backward_block(): jnp.einsum('kbw,bkc->wc', selector, column_grad, precision=lax.Precision....  57.4 us
    reduce_scatter x1, waiting for transfers between devices, per_device(): lax.psum_scatter(partial_x, 'by', scatter_dimension=2, tiled=True)  27 us
    dot_general x2, matrix products, forward_block(): jnp.einsum('kbw,wc->bkc', selector, window, preferred_element_type=jnp.fl...  25.9 us
    ppermute x4, waiting for transfers between devices, extended(): lax.ppermute(head, axis, [((i + 1) % count, i) for i in range(ends)])  12.1 us
  transfers between devices with their start and end apart: 10, of which 6 were waited for; matrix products, arithmetic and copies ran while one was open for 2% of the time, Pallas kernels for 0%

commit v1 on v0

--- a/solution.py
+++ b/solution.py
@@ -88,7 +88,10 @@
     )
     center = total_sum / total_count
     deviation = (conv_float - center) * live_mask
-    variance = lax.psum(jnp.sum(deviation * deviation, axis=0), ("bx", "by")) / total_count
+    variance = (
+        jnp.sum(lax.all_gather(jnp.sum(deviation * deviation, axis=0), ("bx", "by")), axis=0)
+        / total_count
+    )
     inverse_std = lax.rsqrt(variance + epsilon)
     normalized = (conv_float - center) * inverse_std
     before = gain * normalized + shift

time: 466 us -> 433 us (0.929)
  blocking collectives: 197 us -> 163 us
    psum x1 -> x0, blocking collectives: 62.7 us -> none  [per_device(): lax.psum(jnp.sum(deviation * deviation, axis=0), ('bx', 'by')) / total_count]
    all_gather x0 -> x1, blocking collectives: none -> 28.7 us  [per_device(): lax.all_gather(jnp.sum(deviation * deviation, axis=0), ('bx', 'by'))]
where the time goes in v1:
time: 433 us; the launch traced here: 432 us
  blocking collectives  163 us (38%)
  waiting for transfers between devices  103 us (24%)
  matrix products  99.4 us (23%)
  between operations  16.4 us (4%)
  local copies, waits for them, and re-layouts  15.4 us (4%)
  starting transfers between devices  14.8 us (3%)
  other arithmetic  13.8 us (3%)
  loops' own time  5.44 us (1%)
    psum x1, blocking collectives, per_device(): lax.psum((jnp.sum(conv_float * live_mask, axis=0), local_count), ('bx', '...  70.3 us
    unnamed x3, waiting for transfers between devices  64.7 us
    psum x1, blocking collectives, per_device(): lax.psum((jnp.sum(upstream, axis=0), jnp.sum(upstream * normalized, axis=...  64 us
    dot_general x2, matrix products, backward_block(): jnp.einsum('kbw,bkc->wc', selector, column_grad, precision=lax.Precision....  57.4 us
    all_gather x1, blocking collectives, per_device(): lax.all_gather(jnp.sum(deviation * deviation, axis=0), ('bx', 'by'))  28.7 us
    reduce_scatter x1, waiting for transfers between devices, per_device(): lax.psum_scatter(partial_x, 'by', scatter_dimension=2, tiled=True)  27 us
    dot_general x2, matrix products, forward_block(): jnp.einsum('kbw,wc->bkc', selector, window, preferred_element_type=jnp.fl...  25.9 us
    ppermute x4, waiting for transfers between devices, extended(): lax.ppermute(head, axis, [((i + 1) % count, i) for i in range(ends)])  11.6 us
  transfers between devices with their start and end apart: 10, of which 6 were waited for; matrix products, arithmetic and copies ran while one was open for 2% of the time, Pallas kernels for 0%

profile of v1, /device:TPU:0, one launch (start us, length us, event | category | flops | bytes accessed | tf_op | source)
XLA Modules:
  0.0 431.7 jit_solution(18226685468647096655)
XLA Ops:
  7.2 1.9 fusion.34
  9.1 3.9 collective-permute-start
  13.0 1.3 collective-permute-start.1
  15.2 4.3 %collective-permute-done.1 = bf16[1,3,128,128]{3,2,1,0:T(8,128)(2,1)S(1)} collective-permute-done((bf16[1,3,128,128]{3,2,1,0:T(8,128)(2,1)S(1)}, bf16[1,3,128,128]{3,2,1,0:T(8,128)(2,1)S(1)}, u32[]{:S(2)}, u32[]{:S(2)}) %collective-permute-start.1) | collective-permute-done | bytes 98336 | tf_op jit(solution)/shard_map/ppermute | solution.py:19
  19.5 0.8 pad_maximum_fusion.9
  20.3 1.9 collective-permute-start.2
  22.2 1.3 collective-permute-start.3
  23.6 1.2 reduce.5
  24.9 0.6 fusion.44
  25.5 1.5 collective-permute-done.3
  27.0 1.1 pad_maximum_fusion
  28.2 38.2 %while.33 = (s32[]{:T(128)}, bf16[2,512,128]{2,1,0:T(8,128)(2,1)S(1)}, bf16[2,512,3456]{1,2,0:T(8,128)(2,1)}, bf16[2,512,128]{2,1,0:T(8,128)(2,1)}, bf16[2,9,64,...) while((s32[]{:T(128)}, ...), condition=%wide.region_1.2_spmd.clone, body=%wide.region_0.1_spmd.sunk.clone | while | flops 4321123840 | bytes 16304801 | solution.py:77
  28.2 0.6 dynamic_slice.94
  30.2 0.9 dynamic-slice_bitcast_fusion.3
  31.2 13.0 %fusion.82 = bf16[128,27,512]{2,0,1:T(8,128)(2,1)S(1)} fusion(s32[27,512]{1,0:T(8,128)S(1)} %bitcast_select_fusion.6, bf16[576,128]{1,0:T(8,128)(2,1)S(1)} %bitcast.224, bf16[512,128]{1,0:T(8,128)(2,1)S(1)} %dynamic-slice_bitcast_fusion.3), kind=kOutput, calls=%fused_computation.3.clone.1.clone | convolution fusion | flops 3867738112 | bytes 3872768 | tf_op jit(solution)/shard_map/while/body/eval_jaxpr/kbw,wc->bkc/dot_general | solution.py:71
  44.1 2.0 constant_dynamic-update-slice_fusion.6
  46.1 1.2 fusion.83
  47.3 0.6 dynamic_slice.94
  49.3 0.9 dynamic-slice_bitcast_fusion.3
  50.2 13.0 %fusion.82 = bf16[128,27,512]{2,0,1:T(8,128)(2,1)S(1)} fusion(s32[27,512]{1,0:T(8,128)S(1)} %bitcast_select_fusion.6, bf16[576,128]{1,0:T(8,128)(2,1)S(1)} %bitcast.224, bf16[512,128]{1,0:T(8,128)(2,1)S(1)} %dynamic-slice_bitcast_fusion.3), kind=kOutput, calls=%fused_computation.3.clone.1.clone | convolution fusion | flops 3867738112 | bytes 3872768 | tf_op jit(solution)/shard_map/while/body/eval_jaxpr/kbw,wc->bkc/dot_general | solution.py:71
  63.2 2.0 constant_dynamic-update-slice_fusion.6
  65.2 1.2 fusion.83
  66.4 0.2 multiply_reduce_fusion.1
  66.6 70.3 %all-reduce.2 = (f32[128]{0:T(128)S(1)}, f32[]{:T(128)}) all-reduce(f32[128]{0:T(128)S(1)} %multiply_reduce_fusion.1, f32[]{:T(128)} %fusion.44), channel_id=1, replica_groups=mesh['bx'=16,'by'=8] {'bx','by'}, use_global_device_ids=true, to_apply=%region_3.4 | all-reduce | flops 129 | bytes 1032 | tf_op jit(solution)/shard_map/psum | solution.py:86
  136.9 0.7 broadcast_divide_fusion
  137.6 0.2 multiply_reduce_fusion
  137.8 28.7 %all-gather.1 = f32[128,1,128]{2,1,0:T(1,128)S(1)} all-gather(f32[1,1,128]{2,1,0:T(1,128)S(1)} %bitcast.241), channel_id=2, replica_groups=mesh['bx'=16,'by'=8] {'bx','by'}, dimensions={0}, use_global_device_ids=true | all-gather | bytes 66048 | tf_op jit(solution)/shard_map/all_gather | solution.py:92
  166.5 0.2 reduce_sum.57
  166.7 0.7 fusion.46
  167.4 1.2 fusion.39
  168.5 64.0 %all-reduce.1 = (f32[128]{0:T(128)S(1)}, f32[128]{0:T(128)S(1)}) all-reduce(f32[128]{0:T(128)S(1)} %get-tuple-element.329, f32[128]{0:T(128)S(1)} %get-tuple-element.328), channel_id=1, replica_groups=mesh['bx'=16,'by'=8] {'bx','by'}, use_global_device_ids=true, to_apply=%region_11.12 | all-reduce | flops 256 | bytes 2048 | tf_op jit(solution)/shard_map/psum | solution.py:100
  232.5 1.9 fusion.42
  234.4 73.1 %while.34 = (s32[]{:T(128)}, f32[3456,128]{1,0:T(8,128)S(1)}, f32[2,512,128]{2,1,0:T(8,128)}, bf16[2,9,64,128]{3,2,0,1:T(8,128)(2,1)}, bf16[2,512,3456]{1,2,0:T(...) while((s32[]{:T(128)}, f32[3456,128]{1,0:T(8,128)S(1)}, ...), condition=%wide.region_13.14_spmd.clone.clone, body=%wide.region_12.13_spmd.clone.sunk.clone | while | flops 24024522752 | bytes 28413672 | solution.py:133
  234.4 0.6 dynamic_slice.99
  236.4 1.1 fusion.89
  237.5 28.7 %fusion.90 = f32[1088,128]{1,0:T(8,128)S(1)} fusion(f32[512,27,128]{2,0,1:T(8,128)S(1)} %fusion.89, s32[27,512]{1,0:T(8,128)S(1)} %bitcast_select_fusion.7), kind=kOutput, calls=%fused_computation.31.clone.1.clone | convolution fusion | flops 23117266944 | bytes 7690240 | tf_op jit(solution)/shard_map/while/body/eval_jaxpr/kbw,bkc->wc/dot_general | solution.py:120
  266.3 0.8 copy-done.4
  267.1 0.7 constant_dynamic-update-slice_fusion.7
  267.8 3.2 convolution_add_fusion.3
  271.0 0.6 dynamic_slice.99
  273.0 1.1 fusion.89
  274.1 28.7 %fusion.90 = f32[1088,128]{1,0:T(8,128)S(1)} fusion(f32[512,27,128]{2,0,1:T(8,128)S(1)} %fusion.89, s32[27,512]{1,0:T(8,128)S(1)} %bitcast_select_fusion.7), kind=kOutput, calls=%fused_computation.31.clone.1.clone | convolution fusion | flops 23117266944 | bytes 7690240 | tf_op jit(solution)/shard_map/while/body/eval_jaxpr/kbw,bkc->wc/dot_general | solution.py:120
  302.9 0.8 copy-done.4
  303.6 0.7 constant_dynamic-update-slice_fusion.7
  304.3 3.2 convolution_add_fusion.3
  307.6 1.0 convert_element_type.131
  308.7 1.0 fusion.48
  309.6 2.4 collective-permute-start.4
  312.0 1.3 collective-permute-start.5
  313.3 0.6 dynamic-slice
  315.3 3.6 collective-permute-done.5
  318.9 1.0 pad_maximum_fusion.6
  319.9 1.4 collective-permute-start.6
  321.2 1.3 collective-permute-start.7
  322.5 0.9 multiply_convert_fusion
  323.4 2.1 collective-permute-done.7
  325.6 1.1 pad_maximum_fusion.1
  326.8 64.7 %all-reduce.5.cloned.1.call-done = bf16[27,128,128]{2,1,0:T(8,128)(2,1)} async-done(((bf16[27,128,128]{2,1,0:T(8,128)(2,1)}), bf16[27,128,128]{2,1,0:T(8,128)(2,1)}) %all-reduce.5.cloned.1.call-update) | async-done | bytes 884752
  391.5 0.8 constant_dynamic-slice_fusion.1
  392.3 0.9 copy.30
  393.2 3.2 fusion.35
  396.4 27.0 %reduce-scatter.3.cloned.1.call-done = bf16[27,8,16]{0,1,2:T(8,128)(2,1)} async-done(((bf16[27,8,128]{0,1,2:T(8,128)(2,1)}), bf16[27,8,16]{0,1,2:T(8,128)(2,1)}) %reduce-scatter.3.cloned.1.call-update) | async-done | bytes 6928 | tf_op jit(solution)/shard_map/reduce_scatter | solution.py:140
  423.4 0.8 convert_divide_fusion
  424.2 0.6 copy.31
  (53 shorter events, 1.1 us)
Async XLA Ops:
  7.2 21.0 %copy-start = (bf16[3456,128]{1,0:T(8,128)(2,1)S(1)}, bf16[3456,128]{1,0:T(8,128)(2,1)}, u32[]{:S(2)}) copy-start(bf16[3456,128]{1,0:T(8,128)(2,1)} %param.16) | copy-start | bytes 2654212
  7.2 384.3 %all-reduce.5.cloned.1.call-start = ((), (), s32[]{:S(2)}) async-start(), calls=%async_computation.2 | async-start | bytes 1769472
  9.1 6.1 %collective-permute-start = (bf16[1,3,128,128]{3,2,1,0:T(8,128)(2,1)S(1)}, bf16[1,3,128,128]{3,2,1,0:T(8,128)(2,1)S(1)}, u32[]{:S(2)}, u32[]{:S(2)}) collective-permute-start(bf16[1,3,128,128]{3,2,1,0:T(8,128)(2,1)S(1)} %bitcast.240), channel_id=1, source_target_pairs={{0,8},{8,16},{16,24},{24,32},{32,40},{40,48},{48,56},{56,64},{64,7... | collective-permute-start | bytes 294920 | tf_op jit(solution)/shard_map/ppermute | solution.py:17
  13.0 6.5 %collective-permute-start.1 = (bf16[1,3,128,128]{3,2,1,0:T(8,128)(2,1)S(1)}, bf16[1,3,128,128]{3,2,1,0:T(8,128)(2,1)S(1)}, u32[]{:S(2)}, u32[]{:S(2)}) collective-permute-start(bf16[1,3,128,128]{3,2,1,0:T(8,128)(2,1)S(1)} %bitcast.239), channel_id=1, source_target_pairs={{8,0},{16,8},{24,16},{32,24},{40,32},{48,40},{56,48},{64,56},{72,6... | collective-permute-start | bytes 294920 | tf_op jit(solution)/shard_map/ppermute | solution.py:19
  20.3 5.2 %collective-permute-start.2 = (bf16[5,1,128,128]{3,2,1,0:T(8,128)(2,1)}, bf16[5,1,128,128]{3,2,1,0:T(8,128)(2,1)}, u32[]{:S(2)}, u32[]{:S(2)}) collective-permute-start(bf16[5,1,128,128]{3,2,1,0:T(8,128)(2,1)} %get-tuple-element.372), channel_id=1, source_target_pairs={{0,1},{1,2},{2,3},{3,4},{4,5},{5,6},{6,7},{8,9},{9,10},{10,11},{11... | collective-permute-start | bytes 491528 | tf_op jit(solution)/shard_map/ppermute | solution.py:17
  22.2 4.8 %collective-permute-start.3 = (bf16[5,1,128,128]{3,2,1,0:T(8,128)(2,1)}, bf16[5,1,128,128]{3,2,1,0:T(8,128)(2,1)}, u32[]{:S(2)}, u32[]{:S(2)}) collective-permute-start(bf16[5,1,128,128]{3,2,1,0:T(8,128)(2,1)} %get-tuple-element.373), channel_id=1, source_target_pairs={{1,0},{2,1},{3,2},{4,3},{5,4},{6,5},{7,6},{9,8},{10,9},{11,10},{12... | collective-permute-start | bytes 491528 | tf_op jit(solution)/shard_map/ppermute | solution.py:19
  28.2 138.5 %copy-start.1 = (f32[128]{0:T(128)S(1)}, f32[128]{0:T(128)}, u32[]{:S(2)}) copy-start(f32[128]{0:T(128)} %param.17) | copy-start | bytes 1540
  28.2 139.1 %copy-start.2 = (f32[128]{0:T(128)S(1)}, f32[128]{0:T(128)}, u32[]{:S(2)}) copy-start(f32[128]{0:T(128)} %param.18) | copy-start | bytes 1540
  234.4 78.9 %copy-start.6 = (u32[128]{0:T(128)S(1)}, u32[128]{0:T(128)}, u32[]{:S(2)}) copy-start(u32[128]{0:T(128)} %constant.182) | copy-start | bytes 1540
  237.5 28.7 %copy-start.3 = (f32[2,512,128]{2,1,0:T(8,128)S(1)}, f32[2,512,128]{2,1,0:T(8,128)}, u32[]{:S(2)}) copy-start(f32[2,512,128]{2,1,0:T(8,128)} %get-tuple-element.580) | copy-start | bytes 1572868 | tf_op jit(solution)/shard_map/while
  266.3 0.8 copy-start.4
  274.1 28.7 %copy-start.3 = (f32[2,512,128]{2,1,0:T(8,128)S(1)}, f32[2,512,128]{2,1,0:T(8,128)}, u32[]{:S(2)}) copy-start(f32[2,512,128]{2,1,0:T(8,128)} %get-tuple-element.580) | copy-start | bytes 1572868 | tf_op jit(solution)/shard_map/while
  302.8 0.8 copy-start.4
  307.6 85.7 %copy-start.5 = (s32[1,1,8,128]{3,2,1,0:T(8,128)S(1)}, s32[1,1,8,128]{3,2,1,0:T(8,128)}, u32[]{:S(2)}) copy-start(s32[1,1,8,128]{3,2,1,0:T(8,128)} %param.15) | copy-start | bytes 12292
  308.6 114.8 %reduce-scatter.3.cloned.1.call-start = ((), (), s32[]{:S(2)}) async-start(), calls=%async_computation.1 | async-start | bytes 294912 | tf_op jit(solution)/shard_map/reduce_scatter | solution.py:140
  309.6 5.6 %collective-permute-start.4 = (bf16[1,3,128,128]{3,2,1,0:T(8,128)(2,1)S(1)}, bf16[1,3,128,128]{3,2,1,0:T(8,128)(2,1)S(1)}, u32[]{:S(2)}, u32[]{:S(2)}) collective-permute-start(bf16[1,3,128,128]{3,2,1,0:T(8,128)(2,1)S(1)} %bitcast.238), channel_id=1, source_target_pairs={{0,8},{8,16},{16,24},{24,32},{32,40},{40,48},{48,56},{56,64},{64,7... | collective-permute-start | bytes 294920 | tf_op jit(solution)/shard_map/ppermute | solution.py:17
  312.0 6.9 %collective-permute-start.5 = (bf16[1,3,128,128]{3,2,1,0:T(8,128)(2,1)S(1)}, bf16[1,3,128,128]{3,2,1,0:T(8,128)(2,1)S(1)}, u32[]{:S(2)}, u32[]{:S(2)}) collective-permute-start(bf16[1,3,128,128]{3,2,1,0:T(8,128)(2,1)S(1)} %bitcast.237), channel_id=1, source_target_pairs={{8,0},{16,8},{24,16},{32,24},{40,32},{48,40},{56,48},{64,56},{72,6... | collective-permute-start | bytes 294920 | tf_op jit(solution)/shard_map/ppermute | solution.py:19
  319.9 3.6 collective-permute-start.6
  321.2 4.4 %collective-permute-start.7 = (bf16[5,1,128,128]{3,2,1,0:T(8,128)(2,1)S(1)}, bf16[5,1,128,128]{3,2,1,0:T(8,128)(2,1)S(1)}, u32[]{:S(2)}, u32[]{:S(2)}) collective-permute-start(bf16[5,1,128,128]{3,2,1,0:T(8,128)(2,1)S(1)} %get-tuple-element.371), channel_id=1, source_target_pairs={{1,0},{2,1},{3,2},{4,3},{5,4},{6,5},{7,6},{9,8},{10,9},{11,10},{12... | collective-permute-start | bytes 491528 | tf_op jit(solution)/shard_map/ppermute | solution.py:19
Sparse Core Ops, SparseCore 0:
  308.8 82.6 all-reduce.4
  393.8 29.5 reduce-scatter.2
